TPU v7x, 512 devices: a whole 4x8x8 slice. The times are simulated.
512 devices in a mesh: seq: 64 (over x, y, core), head: 8 (over z).
Axes of the slice: x: 4, y: 8, z: 8, core: 2. Of those that a mesh axis runs over, the one named last changes fastest.
Arguments:
- queries: bfloat16 [69632, 2048], P('seq', 'head'), may hold values from -50 to 50
- keys: bfloat16 [69632, 2048], P('seq', 'head'), may hold values from -6 to 6
- values: bfloat16 [69632, 2048], P('seq', 'head'), may hold values from -48 to 48
- rand_group: int32 [1088, 3], replicated, may hold values from 0 to 63, all different within a row; in each aligned block of 17 rows (0 to 16, 17 to 33, ...) at most 2 rows name the same one
- rand_offset: int32 [1088, 3], replicated, may hold values from 0 to 16
- glob_blocks: int32 [2], replicated, may hold values from 0 to 1087
- w_out: bfloat16 [2048, 4096], P(None, 'head'), may hold values from -0.125 to 0.125
Outputs:
- layer_out: bfloat16 [69632, 4096], P('seq', 'head')
Inputs may be any that keep to these rules, and one draw needn't show every extreme that they name: `rand_group`: each row names 3 different groups. Among the 17 rows of one aligned block of 17 rows, no group is named more than 2 times, and in every draw some group is named exactly 2 times in some such block.
All inputs are finite; a program needn't handle non-finite values.
Results may differ from a plain program's by a relative error of at most 0.0056.
Values may be sent and summed in bfloat16 or wider, within the bound.
A program may use at most 128 MiB of HBM per device.

v0:
```python
from functools import reduce
import math
import jax
import jax.numpy as jnp
from jax import lax
from jax.sharding import PartitionSpec as P

DH = 128
BLOCK = 64
R = 3
G = 2


def padded_2(x, sides, width):
    for axis, dim in sides:
        size, length = (lax.axis_size(axis), x.shape[dim])
        up = [(i, (i + 1) % size) for i in range(size)]
        down = [(j, i) for i, j in up]
        last = lax.slice_in_dim(x, length - width, length, axis=dim)
        initial = lax.slice_in_dim(x, 0, width, axis=dim)
        before = lax.ppermute(last, axis, up)
        after = lax.ppermute(initial, axis, down)
        x = jnp.concatenate([before, x, after], axis=dim)
    return x


def spread(block, axis, holder):
    block = jnp.where(lax.axis_index(axis) == holder, block, jnp.zeros_like(block))
    return lax.psum(block, axis)


def attend_sets(query_rows, pair_sets, columns):
    head_count = columns // DH
    block_count = query_rows.shape[0]
    query_heads = query_rows.reshape(block_count, BLOCK, head_count, DH)
    score_scale = 1.0 / math.sqrt(DH)
    score_list = []
    for pair_rows in pair_sets:
        key_part = pair_rows[..., :columns].reshape(block_count, -1, head_count, DH)
        score_list.append(
            jnp.einsum("nqhd,nkhd->nhqk", query_heads, key_part, preferred_element_type=jnp.float32)
            * score_scale
        )
    row_max = reduce(
        jnp.maximum, [jnp.max(score_part, axis=-1, keepdims=True) for score_part in score_list]
    )
    row_total = jnp.zeros((block_count, head_count, BLOCK), jnp.float32)
    weighted = jnp.zeros((block_count, BLOCK, head_count, DH), jnp.float32)
    for score_part, pair_rows in zip(score_list, pair_sets):
        weights = jnp.exp(score_part - row_max)
        row_total = jnp.sum(weights, axis=-1)
        value_part = pair_rows[..., columns:].reshape(block_count, -1, head_count, DH)
        weighted = jnp.einsum(
            "nhqk,nkhd->nqhd",
            weights.astype(jnp.bfloat16),
            value_part,
            preferred_element_type=jnp.float32,
        )
    context = weighted / jnp.transpose(row_total, (0, 2, 1))[..., None]
    return context.astype(jnp.bfloat16).reshape(block_count * BLOCK, columns)


def on_device(queries, keys, values, rand_group, rand_offset, glob_blocks, w_out):
    columns = queries.shape[1]
    tokens_dev = queries.shape[0]
    per_device = tokens_dev // BLOCK
    seq_count = lax.axis_size("seq")
    my_index = lax.axis_index("seq")
    slot_cap = rand_group.shape[0] // seq_count * R
    slot_cap = max(2, (slot_cap + seq_count - 1) // seq_count)
    pair_rows = jnp.concatenate([keys, values], axis=1)
    pair_blocks = pair_rows.reshape(per_device, BLOCK, 2 * columns)
    padded = padded_2(pair_rows, (("seq", 0),), BLOCK)
    padded_blocks = padded.reshape(per_device + 2, BLOCK, 2 * columns)
    window_sets = jnp.stack([padded_blocks[:-2], padded_blocks[1:-1], padded_blocks[2:]], axis=1)
    found = []
    for global_slot in range(G):
        owner_index = glob_blocks[global_slot] // per_device
        local_spot = glob_blocks[global_slot] % per_device
        piece_rows = lax.dynamic_index_in_dim(pair_blocks, local_spot, 0, keepdims=False)
        found.append(spread(piece_rows, "seq", owner_index))
    global_pairs = jnp.stack(found)
    global_sets = jnp.broadcast_to(global_pairs[None], (per_device, G, BLOCK, 2 * columns))
    request_count = per_device * R
    asked_groups = rand_group.reshape(seq_count, request_count)
    asked_offsets = rand_offset.reshape(seq_count, request_count)
    asked_here = (asked_groups == my_index).astype(jnp.int32)
    slot_rank = jnp.cumsum(asked_here, axis=1) - asked_here
    slot_index = jnp.arange(slot_cap, dtype=jnp.int32)
    slot_match = (asked_here[:, None, :] == 1) & (
        slot_rank[:, None, :] == slot_index[None, :, None]
    )
    send_spot = jnp.sum(jnp.where(slot_match, asked_offsets[:, None, :], 0), axis=2)
    slot_filled = jnp.any(slot_match, axis=2)
    outgoing = jnp.take(pair_blocks, send_spot.reshape(-1), axis=0).reshape(
        seq_count, slot_cap, BLOCK, 2 * columns
    )
    outgoing = jnp.where(slot_filled[:, :, None, None], outgoing, jnp.zeros_like(outgoing))
    incoming = lax.all_to_all(outgoing, "seq", split_axis=0, concat_axis=0, tiled=True)
    my_groups = lax.dynamic_slice_in_dim(rand_group, my_index * per_device, per_device, 0).reshape(
        -1
    )
    request_index = jnp.arange(request_count, dtype=jnp.int32)
    earlier_same = (my_groups[None, :] == my_groups[:, None]) & (
        request_index[None, :] < request_index[:, None]
    )
    arrival_rank = jnp.sum(earlier_same.astype(jnp.int32), axis=1)
    arrival_spot = my_groups * slot_cap + arrival_rank
    random_sets = jnp.take(
        incoming.reshape(seq_count * slot_cap, BLOCK, 2 * columns), arrival_spot, axis=0
    )
    random_sets = random_sets.reshape(per_device, R, BLOCK, 2 * columns)
    query_rows = queries.reshape(per_device, BLOCK, columns)
    joined_sets = jnp.concatenate([window_sets, global_sets, random_sets], axis=1).reshape(
        per_device, -1, 2 * columns
    )
    context = attend_sets(query_rows, [joined_sets], columns)
    summed = jnp.dot(
        lax.all_gather(context, "head", axis=1, tiled=True),
        w_out,
        preferred_element_type=jnp.float32,
    )
    return summed.astype(jnp.bfloat16)


def solution(mesh):
    return jax.shard_map(
        on_device,
        mesh=mesh,
        in_specs=(
            P("seq", "head"),
            P("seq", "head"),
            P("seq", "head"),
            P(),
            P(),
            P(),
            P(None, "head"),
        ),
        out_specs=P("seq", "head"),
        check_vma=False,
    )
```

profile of v0, /device:TPU:64, one launch (start us, length us, event | category | flops | bytes accessed | tf_op | source)
XLA Modules:
  0.0 396.6 jit_solution(1737452305502771908)
XLA Ops:
  6.5 0.9 compare_convert_fusion
  7.4 0.2 copy.53
  7.7 0.2 reshape.172
  7.9 0.2 reduce_window_sum.11
  8.2 0.1 copy.54
  8.3 1.0 copy.58
  9.3 0.2 broadcast_in_dim.62
  9.6 0.1 copy.61
  9.8 1.1 constant_dynamic-update-slice_fusion.1
  10.9 0.1 reshape.164
  11.1 0.1 copy.60
  11.2 0.1 copy.57
  11.3 1.1 constant_dynamic-update-slice_fusion
  12.4 6.4 %gather_fusion = bf16[128,64,512]{2,1,0:T(8,128)(2,1)} fusion(bf16[17,64,512]{2,1,0:T(8,128)(2,1)S(1)} %bitcast.52, s32[1024]{0:T(1024)S(1)} %pad_clamp_fusion.1), kind=kCustom, calls=%fused_computation | custom fusion | bytes 16777728 | tf_op jit(solution)/shard_map/jit(_take)/gather | solution.py:95
  18.8 7.5 %select_select_fusion = bf16[64,2,64,512]{3,2,1,0:T(8,128)(2,1)} fusion(bf16[64,2,64,512]{3,2,1,0:T(8,128)(2,1)} %bitcast.55, pred[64,2]{1,0:T(8,128)(4,1)S(1)} %copy.60, pred[64,2]{1,0:T(8,128)(4,1)S(1)} %copy.57), kind=kLoop, calls=%fused_computation.2 | loop fusion | flops 8388608 | bytes 16777472 | tf_op jit(solution)/shard_map/jit(_where)/select_n | solution.py:98
  26.3 10.9 %all-to-all-start = ((bf16[64,2,64,512]{3,2,1,0:T(8,128)(2,1)}), bf16[64,2,64,512]{3,2,1,0:T(8,128)(2,1)}, u32[]{:S(2)}, u32[]{:S(2)}) async-start(bf16[64,2,64,512]{3,2,1,0:T(8,128)(2,1)} %select_select_fusion), calls=%async_computation | async-start | bytes 16777216 | tf_op jit(solution)/shard_map/all_to_all | solution.py:99
  37.3 1.9 collective-permute-start
  39.2 7.0 %collective-permute-start.1 = (bf16[64,512]{1,0:T(8,128)(2,1)S(1)}, bf16[64,512]{1,0:T(8,128)(2,1)S(1)}, u32[]{:S(2)}, u32[]{:S(2)}) collective-permute-start(bf16[64,512]{1,0:T(8,128)(2,1)S(1)} %get-tuple-element.15), channel_id=1, source_target_pairs={{8,0},{16,8},{24,16},{32,24},{40,32},{48,40},{56,48},{64,56},{72,6... | collective-permute-start | bytes 196616 | tf_op jit(solution)/shard_map/ppermute | solution.py:22
  46.2 0.6 fusion.21
  50.5 0.7 dynamic-slice_select_fusion.1
  51.2 0.2 all-gather.2.cloned.1.call-start
  51.4 0.8 broadcast_multiply_fusion
  52.2 0.1 copy.50
  52.4 0.1 copy.62
  52.5 0.1 mul.34
  52.6 0.2 convert_reduce_fusion
  52.8 0.1 copy.51
  52.9 0.1 copy.52
  53.0 2.5 reshape_reshape.3
  55.5 213.7 %all-reduce.3.cloned.1.call-done = (bf16[1,64,512]{2,1,0:T(8,128)(2,1)}, bf16[1,64,512]{2,1,0:T(8,128)(2,1)}) async-done(((bf16[1,64,512]{2,1,0:T(8,128)(2,1)}, bf16[1,64,512]{2,1,0:T(8,128)(2,1)}), (bf16[1,64,512]{2,1,0:T(8,128)(2,1)}, bf16[1,64,512]{2,1,0:T(8,128)(2,1)})) %all-reduce.3.cloned.1.call-update) | async-done | bytes 131088 | tf_op jit(solution)/shard_map/psum | solution.py:29
  269.2 0.9 pad_maximum_fusion.2
  270.1 0.2 pad_maximum_fusion
  270.3 1.1 constant_dynamic-update-slice_fusion.4
  271.4 1.1 constant_dynamic-update-slice_fusion.3
  272.4 1.1 constant_dynamic-update-slice_fusion.2
  273.5 1.7 broadcast_dynamic-update-slice_fusion
  275.2 5.9 %gather_fusion.1 = bf16[51,64,512]{2,1,0:T(8,128)(2,1)} fusion(bf16[128,64,512]{2,1,0:T(8,128)(2,1)} %bitcast.12, s32[1024]{0:T(1024)S(1)} %pad_clamp_fusion), kind=kCustom, calls=%fused_computation.1 | custom fusion | bytes 6684876 | tf_op jit(solution)/shard_map/jit(_take)/gather | solution.py:109
  281.1 5.2 %select_dynamic-update-slice_fusion = bf16[17,8,64,512]{3,2,1,0:T(8,128)(2,1)} fusion(bf16[17,8,64,512]{3,2,1,0:T(8,128)(2,1)} %broadcast_dynamic-update-slice_fusion, bf16[17,3,64,512]{3,2,1,0:T(8,128)(2,1)} %bitcast.57, pred[17,3]{1,0:T(8,128)(4,1)S(1)} %copy.52), kind=kLoop, calls=%fused_computation.8 | loop fusion | flops 1671168 | bytes 6684723 | tf_op jit(solution)/shard_map/concatenate | solution.py:114
  286.2 8.1 %fusion.19 = (bf16[17,512,256]{2,1,0:T(8,128)(2,1)}, bf16[17,512,256]{2,1,0:T(8,128)(2,1)}) fusion(bf16[17,512,512]{2,1,0:T(8,128)(2,1)} %bitcast.16), kind=kLoop, calls=%fused_computation.51 | loop fusion | bytes 17825792 | tf_op jit(solution)/shard_map/slice | solution.py:39
  294.3 6.5 %copy.64 = bf16[17,512,256]{1,2,0:T(8,128)(2,1)} copy(bf16[17,512,256]{2,1,0:T(8,128)(2,1)} %get-tuple-element.9) | data formatting | bytes 8912896 | tf_op jit(solution)/shard_map/slice | solution.py:39
  300.8 6.6 %copy.63 = bf16[17,512,256]{1,2,0:T(8,128)(2,1)} copy(bf16[17,512,256]{2,1,0:T(8,128)(2,1)} %get-tuple-element.10) | data formatting | bytes 8912896 | tf_op jit(solution)/shard_map/slice | solution.py:52
  307.5 3.4 bitcast_reduce_fusion
  310.9 1.3 fusion.1
  312.2 2.0 divide_convert_fusion
  314.3 0.6 copy.68
  314.8 0.9 copy.78
  315.8 68.3 %all-gather.2.cloned.1.call-done = bf16[1088,2048]{1,0:T(8,128)(2,1)} async-done(((bf16[1088,256]{1,0:T(8,128)(2,1)}), bf16[1088,2048]{1,0:T(8,128)(2,1)}) %all-gather.2.cloned.1.call-update) | async-done | bytes 4456464 | tf_op jit(solution)/shard_map/all_gather | solution.py:119
  384.1 5.7 %convolution_convert_fusion = bf16[1088,512]{1,0:T(8,128)(2,1)} fusion(bf16[1088,2048]{1,0:T(8,128)(2,1)} %all-gather.2.cloned.1.call-done, bf16[2048,512]{1,0:T(8,128)(2,1)S(1)} %copy-done), kind=kOutput, calls=%fused_computation.9 | convolution fusion | flops 2282258432 | bytes 7667712 | tf_op jit(solution)/shard_map/dot_general | solution.py:118
  (32 shorter events, 0.7 us)
Async XLA Ops:
  6.5 377.5 %copy-start = (bf16[2048,512]{1,0:T(8,128)(2,1)S(1)}, bf16[2048,512]{1,0:T(8,128)(2,1)}, u32[]{:S(2)}) copy-start(bf16[2048,512]{1,0:T(8,128)(2,1)} %param.13) | copy-start | bytes 6291460
  26.3 19.9 %copy-start.2 = (s32[2]{0:T(128)S(1)}, s32[2]{0:T(128)}, u32[]{:S(2)}) copy-start(s32[2]{0:T(128)} %param.12) | copy-start | bytes 28
  26.3 248.9 %all-to-all-start = ((bf16[64,2,64,512]{3,2,1,0:T(8,128)(2,1)}), bf16[64,2,64,512]{3,2,1,0:T(8,128)(2,1)}, u32[]{:S(2)}, u32[]{:S(2)}) async-start(bf16[64,2,64,512]{3,2,1,0:T(8,128)(2,1)} %select_select_fusion), calls=%async_computation | async-start | bytes 16777216 | tf_op jit(solution)/shard_map/all_to_all | solution.py:99
  37.2 232.0 %all-reduce.3.cloned.1.call-start = ((), (), s32[]{:S(2)}) async-start(), calls=%async_computation.2 | async-start | bytes 262144 | tf_op jit(solution)/shard_map/psum | solution.py:29
  37.3 232.8 %collective-permute-start = (bf16[64,512]{1,0:T(8,128)(2,1)S(1)}, bf16[64,512]{1,0:T(8,128)(2,1)S(1)}, u32[]{:S(2)}, u32[]{:S(2)}) collective-permute-start(bf16[64,512]{1,0:T(8,128)(2,1)S(1)} %get-tuple-element.16), channel_id=1, source_target_pairs={{0,8},{8,16},{16,24},{24,32},{32,40},{40,48},{48,56},{56,64},{64,7... | collective-permute-start | bytes 196616 | tf_op jit(solution)/shard_map/ppermute | solution.py:21
  39.2 230.9 %collective-permute-start.1 = (bf16[64,512]{1,0:T(8,128)(2,1)S(1)}, bf16[64,512]{1,0:T(8,128)(2,1)S(1)}, u32[]{:S(2)}, u32[]{:S(2)}) collective-permute-start(bf16[64,512]{1,0:T(8,128)(2,1)S(1)} %get-tuple-element.15), channel_id=1, source_target_pairs={{8,0},{16,8},{24,16},{32,24},{40,32},{48,40},{56,48},{64,56},{72,6... | collective-permute-start | bytes 196616 | tf_op jit(solution)/shard_map/ppermute | solution.py:22
  51.2 332.9 %all-gather.2.cloned.1.call-start = ((), (), s32[]{:S(2)}) async-start(), calls=%async_computation.1 | async-start | bytes 5013504 | tf_op jit(solution)/shard_map/all_gather | solution.py:119
  300.8 6.6 %copy-start.1 = (bf16[17,64,2,128]{3,2,1,0:T(2,128)(2,1)S(1)}, bf16[17,64,2,128]{3,2,1,0:T(2,128)(2,1)}, u32[]{:S(2)}) copy-start(bf16[17,64,2,128]{3,2,1,0:T(2,128)(2,1)} %reshape_reshape.3) | copy-start | bytes 1671172
  307.4 4.8 %slice-start = ((s8[4456448]{0:T(1024)(128)(4,1)}), s8[4194304]{0:T(1024)(128)(4,1)S(1)}, s32[]{:S(2)}) async-start(s8[4456448]{0:T(1024)(128)(4,1)} %bitcast.58), calls=%async_computation.3 | async-start | bytes 8388608
  307.5 4.8 %slice-start.1 = ((s8[4456448]{0:T(1024)(128)(4,1)}), s8[262144]{0:T(1024)(128)(4,1)S(1)}, s32[]{:S(2)}) async-start(s8[4456448]{0:T(1024)(128)(4,1)} %bitcast.58), calls=%async_computation.4 | async-start | bytes 524288
Sparse Core Ops, SparseCore 0:
  51.3 217.8 all-reduce.2
  315.9 68.1 all-gather.1
where the time goes:
time: 398 us; the launch traced here: 397 us
  waiting for transfers between devices  282 us (71%)
  local copies, waits for them, and re-layouts  48.1 us (12%)
  starting transfers between devices  20.1 us (5%)
  other arithmetic  17.9 us (4%)
  between operations  17.3 us (4%)
  matrix products  11.2 us (3%)
    psum x1, waiting for transfers between devices, spread(): return lax.psum(block, axis)  214 us
    all_gather x1, waiting for transfers between devices, on_device(): lax.all_gather(context, 'head', axis=1, tiled=True)  68.3 us
    slice x2, local copies, waits for them, and re-layouts, attend_sets(): key_part = pair_rows[..., :columns].reshape(block_count, -1, head_count, DH)  14.6 us
    all_to_all x1, starting transfers between devices, on_device(): lax.all_to_all(outgoing, 'seq', split_axis=0, concat_axis=0, tiled=True)  10.9 us
  transfers between devices with their start and end apart: 5, of which 2 were waited for; matrix products, arithmetic and copies ran while one was open for 3% of the time, Pallas kernels for 0%

commit v1 on v0

--- a/solution.py
+++ b/solution.py
@@ -116,7 +116,9 @@
     )
     context = attend_sets(query_rows, [joined_sets], columns)
     summed = jnp.dot(
-        lax.all_gather(context, "head", axis=1, tiled=True),
+        jnp.concatenate(
+            lax.all_to_all(jnp.stack([context] * lax.axis_size("head")), "head", 0, 0), axis=1
+        ),
         w_out,
         preferred_element_type=jnp.float32,
     )

time: 398 us -> 439 us (1.10)
  the two profiles are of different devices: /device:TPU:64 before, /device:TPU:1 now
where the time goes in v1:
time: 439 us; the launch traced here: 438 us
  waiting for transfers between devices  219 us (50%)
  blocking collectives  109 us (25%)
  local copies, waits for them, and re-layouts  48.3 us (11%)
  other arithmetic  17.9 us (4%)
  starting transfers between devices  17.8 us (4%)
  between operations  17.6 us (4%)
  matrix products  8.89 us (2%)
    psum x1, waiting for transfers between devices, spread(): return lax.psum(block, axis)  219 us
    all_to_all x1, blocking collectives, on_device(): lax.all_to_all(jnp.stack([context] * lax.axis_size('head')), 'head', 0, 0)  109 us
    slice x2, local copies, waits for them, and re-layouts, attend_sets(): key_part = pair_rows[..., :columns].reshape(block_count, -1, head_count, DH)  14.6 us
    all_to_all x1, starting transfers between devices, on_device(): lax.all_to_all(outgoing, 'seq', split_axis=0, concat_axis=0, tiled=True)  12.1 us
  transfers between devices with their start and end apart: 4, of which 1 were waited for; matrix products, arithmetic and copies ran while one was open for 3% of the time, Pallas kernels for 0%

profile of v1, /device:TPU:1, one launch (start us, length us, event | category | flops | bytes accessed | tf_op | source)
XLA Modules:
  0.0 438.3 jit_solution(7799335994730859243)
XLA Ops:
  6.5 0.9 compare_convert_fusion
  7.4 0.2 copy.64
  7.7 0.2 reshape.178
  7.9 0.2 reduce_window_sum.11
  8.2 0.1 copy.65
  8.3 1.0 copy.69
  9.3 0.2 broadcast_in_dim.62
  9.6 0.1 copy.72
  9.8 1.1 constant_dynamic-update-slice_fusion.1
  10.9 0.1 reshape.169
  11.1 0.1 copy.71
  11.2 0.1 copy.68
  11.3 1.1 constant_dynamic-update-slice_fusion
  12.4 6.4 %gather_fusion = bf16[128,64,512]{2,1,0:T(8,128)(2,1)} fusion(bf16[17,64,512]{2,1,0:T(8,128)(2,1)S(1)} %bitcast.55, s32[1024]{0:T(1024)S(1)} %pad_clamp_fusion.1), kind=kCustom, calls=%fused_computation | custom fusion | bytes 16777728 | tf_op jit(solution)/shard_map/jit(_take)/gather | solution.py:95
  18.8 7.5 %select_select_fusion = bf16[64,2,64,512]{3,2,1,0:T(8,128)(2,1)} fusion(bf16[64,2,64,512]{3,2,1,0:T(8,128)(2,1)} %bitcast.58, pred[64,2]{1,0:T(8,128)(4,1)S(1)} %copy.71, pred[64,2]{1,0:T(8,128)(4,1)S(1)} %copy.68), kind=kLoop, calls=%fused_computation.2 | loop fusion | flops 8388608 | bytes 16777472 | tf_op jit(solution)/shard_map/jit(_where)/select_n | solution.py:98
  26.3 12.1 %all-to-all-start = ((bf16[64,2,64,512]{3,2,1,0:T(8,128)(2,1)}), bf16[64,2,64,512]{3,2,1,0:T(8,128)(2,1)}, u32[]{:S(2)}, u32[]{:S(2)}) async-start(bf16[64,2,64,512]{3,2,1,0:T(8,128)(2,1)} %select_select_fusion), calls=%async_computation | async-start | bytes 16777216 | tf_op jit(solution)/shard_map/all_to_all | solution.py:99
  38.5 3.5 collective-permute-start
  42.0 2.1 collective-permute-start.1
  44.2 0.6 fusion.21
  48.7 0.7 dynamic-slice_select_fusion.1
  49.4 0.8 broadcast_multiply_fusion
  50.2 0.1 copy.61
  50.4 0.1 copy.73
  50.5 0.1 mul.34
  50.6 0.2 convert_reduce_fusion
  50.8 0.1 copy.62
  50.9 0.1 copy.63
  51.0 2.5 reshape_reshape.3
  53.5 218.6 %all-reduce.3.cloned.1.call-done = (bf16[1,64,512]{2,1,0:T(8,128)(2,1)}, bf16[1,64,512]{2,1,0:T(8,128)(2,1)}) async-done(((bf16[1,64,512]{2,1,0:T(8,128)(2,1)}, bf16[1,64,512]{2,1,0:T(8,128)(2,1)}), (bf16[1,64,512]{2,1,0:T(8,128)(2,1)}, bf16[1,64,512]{2,1,0:T(8,128)(2,1)})) %all-reduce.3.cloned.1.call-update) | async-done | bytes 131088 | tf_op jit(solution)/shard_map/psum | solution.py:29
  272.2 0.9 pad_maximum_fusion.2
  273.1 0.2 pad_maximum_fusion
  273.2 1.1 constant_dynamic-update-slice_fusion.4
  274.3 1.1 constant_dynamic-update-slice_fusion.3
  275.4 1.1 constant_dynamic-update-slice_fusion.2
  276.5 1.6 broadcast_dynamic-update-slice_fusion
  278.1 5.9 %gather_fusion.1 = bf16[51,64,512]{2,1,0:T(8,128)(2,1)} fusion(bf16[128,64,512]{2,1,0:T(8,128)(2,1)} %bitcast.12, s32[1024]{0:T(1024)S(1)} %pad_clamp_fusion), kind=kCustom, calls=%fused_computation.1 | custom fusion | bytes 6684876 | tf_op jit(solution)/shard_map/jit(_take)/gather | solution.py:109
  284.1 5.1 %select_dynamic-update-slice_fusion = bf16[17,8,64,512]{3,2,1,0:T(8,128)(2,1)} fusion(bf16[17,8,64,512]{3,2,1,0:T(8,128)(2,1)} %broadcast_dynamic-update-slice_fusion, bf16[17,3,64,512]{3,2,1,0:T(8,128)(2,1)} %bitcast.61, pred[17,3]{1,0:T(8,128)(4,1)S(1)} %copy.63), kind=kLoop, calls=%fused_computation.8 | loop fusion | flops 1671168 | bytes 6684723 | tf_op jit(solution)/shard_map/concatenate | solution.py:114
  289.2 8.1 %fusion.19 = (bf16[17,512,256]{2,1,0:T(8,128)(2,1)}, bf16[17,512,256]{2,1,0:T(8,128)(2,1)}) fusion(bf16[17,512,512]{2,1,0:T(8,128)(2,1)} %bitcast.16), kind=kLoop, calls=%fused_computation.51 | loop fusion | bytes 17825792 | tf_op jit(solution)/shard_map/slice | solution.py:39
  297.3 6.5 %copy.75 = bf16[17,512,256]{1,2,0:T(8,128)(2,1)} copy(bf16[17,512,256]{2,1,0:T(8,128)(2,1)} %get-tuple-element.9) | data formatting | bytes 8912896 | tf_op jit(solution)/shard_map/slice | solution.py:39
  303.8 6.6 %copy.74 = bf16[17,512,256]{1,2,0:T(8,128)(2,1)} copy(bf16[17,512,256]{2,1,0:T(8,128)(2,1)} %get-tuple-element.10) | data formatting | bytes 8912896 | tf_op jit(solution)/shard_map/slice | solution.py:52
  310.4 3.4 bitcast_reduce_fusion
  313.8 1.3 fusion.1
  315.2 2.0 divide_convert_fusion
  317.2 0.6 copy.79
  317.9 0.3 stack.27
  318.2 109.2 %all_to_all.10 = bf16[8,1088,256]{2,1,0:T(8,128)(2,1)S(1)} all-to-all(bf16[8,1088,256]{2,1,0:T(8,128)(2,1)S(1)} %stack.27), channel_id=1, replica_groups=mesh['seq'=64,'head'=8] {'head'}, dimensions={0} | all-to-all | bytes 8912896 | tf_op jit(solution)/shard_map/all_to_all | solution.py:120
  427.4 0.6 copy.84
  428.0 3.5 convolution_convert_fusion
  (32 shorter events, 0.7 us)
Async XLA Ops:
  6.5 421.4 %copy-start = (bf16[2048,512]{1,0:T(8,128)(2,1)S(1)}, bf16[2048,512]{1,0:T(8,128)(2,1)}, u32[]{:S(2)}) copy-start(bf16[2048,512]{1,0:T(8,128)(2,1)} %param.13) | copy-start | bytes 6291460
  26.3 17.9 %copy-start.2 = (s32[2]{0:T(128)S(1)}, s32[2]{0:T(128)}, u32[]{:S(2)}) copy-start(s32[2]{0:T(128)} %param.12) | copy-start | bytes 28
  26.3 251.8 %all-to-all-start = ((bf16[64,2,64,512]{3,2,1,0:T(8,128)(2,1)}), bf16[64,2,64,512]{3,2,1,0:T(8,128)(2,1)}, u32[]{:S(2)}, u32[]{:S(2)}) async-start(bf16[64,2,64,512]{3,2,1,0:T(8,128)(2,1)} %select_select_fusion), calls=%async_computation | async-start | bytes 16777216 | tf_op jit(solution)/shard_map/all_to_all | solution.py:99
  38.4 233.7 %all-reduce.3.cloned.1.call-start = ((), (), s32[]{:S(2)}) async-start(), calls=%async_computation.2 | async-start | bytes 262144 | tf_op jit(solution)/shard_map/psum | solution.py:29
  38.5 234.6 %collective-permute-start = (bf16[64,512]{1,0:T(8,128)(2,1)S(1)}, bf16[64,512]{1,0:T(8,128)(2,1)S(1)}, u32[]{:S(2)}, u32[]{:S(2)}) collective-permute-start(bf16[64,512]{1,0:T(8,128)(2,1)S(1)} %get-tuple-element.16), channel_id=1, source_target_pairs={{0,8},{8,16},{16,24},{24,32},{32,40},{40,48},{48,56},{56,64},{64,7... | collective-permute-start | bytes 196616 | tf_op jit(solution)/shard_map/ppermute | solution.py:21
  42.0 231.0 %collective-permute-start.1 = (bf16[64,512]{1,0:T(8,128)(2,1)S(1)}, bf16[64,512]{1,0:T(8,128)(2,1)S(1)}, u32[]{:S(2)}, u32[]{:S(2)}) collective-permute-start(bf16[64,512]{1,0:T(8,128)(2,1)S(1)} %get-tuple-element.15), channel_id=1, source_target_pairs={{8,0},{16,8},{24,16},{32,24},{40,32},{48,40},{56,48},{64,56},{72,6... | collective-permute-start | bytes 196616 | tf_op jit(solution)/shard_map/ppermute | solution.py:22
  303.8 6.6 %copy-start.1 = (bf16[17,64,2,128]{3,2,1,0:T(2,128)(2,1)S(1)}, bf16[17,64,2,128]{3,2,1,0:T(2,128)(2,1)}, u32[]{:S(2)}) copy-start(bf16[17,64,2,128]{3,2,1,0:T(2,128)(2,1)} %reshape_reshape.3) | copy-start | bytes 1671172
  310.4 4.7 %slice-start = ((s8[4456448]{0:T(1024)(128)(4,1)}), s8[4194304]{0:T(1024)(128)(4,1)S(1)}, s32[]{:S(2)}) async-start(s8[4456448]{0:T(1024)(128)(4,1)} %bitcast.62), calls=%async_computation.3 | async-start | bytes 8388608
  310.4 4.8 %slice-start.1 = ((s8[4456448]{0:T(1024)(128)(4,1)}), s8[262144]{0:T(1024)(128)(4,1)S(1)}, s32[]{:S(2)}) async-start(s8[4456448]{0:T(1024)(128)(4,1)} %bitcast.62), calls=%async_computation.4 | async-start | bytes 524288
Sparse Core Ops, SparseCore 0:
  49.5 222.5 all-reduce.2
